TPU v7x, 32 devices: a whole 2x2x4 slice. The times are simulated.
32 devices in a mesh: grp: 2 (over y), leaf: 16 (over z, x, core).
Axes of the slice: x: 2, y: 2, z: 4, core: 2. Of those that a mesh axis runs over, the one named last changes fastest.
Arguments:
- vectors: float32 [16, 32768], P(None, ('grp', 'leaf')), may hold values from -6 to 6
- points: float32 [3, 32768], P(None, ('grp', 'leaf')), may hold values from -1 to 2
- near_lists: int32 [64, 6], P(('grp', 'leaf')), may hold values from -1 to 5, as said below
- inter_lists: int32 [64, 16], P(('grp', 'leaf')), may hold values from 0 to 31, as said below
- skeleton: int32 [64, 64], P(('grp', 'leaf')), may hold values from 0 to 511, as said below
- interp: float32 [64, 64, 512], P(('grp', 'leaf')), may hold values from -0.25 to 0.25
- transfer: float32 [64, 64, 128], P(('grp', 'leaf')), may hold values from -0.125 to 0.125
- coarse_points: float32 [2, 3, 128], replicated, may hold values from 0 to 1
Outputs:
- filtered: float32 [16, 32768], P(None, ('grp', 'leaf'))
Inputs may be any that keep to these rules, and one draw needn't show every extreme that they name: `near_lists`: place w of leaf l's window is leaf (l // 2 - 1) * 2 + w. Slot 0 holds the leaf itself (2 + l % 2); the next slots hold distinct places of other leaves of the same subtree; then -1 to the end of the row. `inter_lists`: distinct leaves of the leaf's own subtree, numbered from the subtree's first leaf, none in the leaf's window. `skeleton`: distinct places within the leaf.
All inputs are finite; a program needn't handle non-finite values.
Results may differ from a plain program's by a relative error of at most 0.00013.
Values sent between devices are 32-bit elements; how exact they have to be, the bound alone decides.
No kernel may reach another device: no remote copies, remote signals or barrier semaphores. Data moves between devices by JAX's collectives and lax.ppermute only.
A program may use at most 64 MiB of HBM per device.

v0:
```python
import jax
import jax.numpy as jnp
from jax import lax
from jax.sharding import PartitionSpec as P

kappa_scale = 3.4641016151377544
centre = 0.05
half_width = 0.05
highest = lax.Precision.HIGHEST


def with_halo(x, sides, width):
    for axis, dim in sides:
        devices, length = (lax.axis_size(axis), x.shape[dim])
        up = [(i, (i + 1) % devices) for i in range(devices - 1)]
        down = [(j, i) for i, j in up]
        last = lax.slice_in_dim(x, length - width, length, axis=dim)
        initial = lax.slice_in_dim(x, 0, width, axis=dim)
        before = lax.ppermute(last, axis, up)
        after = lax.ppermute(initial, axis, down)
        x = jnp.concatenate([before, x, after], axis=dim)
    return x


def matern(source, target):
    delta_x = source[..., 0, :, None] - target[..., 0, None, :]
    delta_y = source[..., 1, :, None] - target[..., 1, None, :]
    delta_z = source[..., 2, :, None] - target[..., 2, None, :]
    scaled = kappa_scale * jnp.sqrt(delta_x * delta_x + delta_y * delta_y + delta_z * delta_z)
    return (1.0 + scaled) * jnp.exp(-scaled)


def on_device(vectors, points, near_lists, inter_lists, skeleton, interp, transfer, coarse_points):
    per_dev = near_lists.shape[0]
    slot_count = near_lists.shape[1]
    leaf_size = interp.shape[2]
    vec_count = vectors.shape[0]
    leaf_index = lax.axis_index("leaf")
    group_index = lax.axis_index("grp")
    group_count = lax.axis_size("grp")
    leaf_points = points.reshape(3, per_dev, leaf_size).transpose(1, 0, 2)
    skel_points = jnp.take_along_axis(leaf_points, skeleton[:, None, :], axis=2)
    subtree_skel = lax.all_gather(skel_points, "leaf", axis=0, tiled=True)
    own_coarse = lax.dynamic_index_in_dim(coarse_points, group_index, 0, keepdims=False)
    apart = (jnp.arange(group_count) != group_index).astype(jnp.float32)
    coupling = matern(coarse_points, own_coarse[None]) * apart[:, None, None]
    live_slots = jnp.max(jnp.sum((near_lists >= 0).astype(jnp.int32), axis=1))
    first_leaf = leaf_index * per_dev
    subtree_lists = lax.all_gather(inter_lists, "leaf", axis=0, tiled=True)
    own_ids = first_leaf + jnp.arange(per_dev, dtype=jnp.int32)
    hits = jnp.sum(
        (subtree_lists[:, :, None] == own_ids[None, None, :]).astype(jnp.float32), axis=1
    )
    push_kernel = matern(skel_points[None], subtree_skel[:, None]) * hits[:, :, None, None]

    def operate(field):
        stacked = jnp.concatenate([points, field], axis=0)
        window = with_halo(stacked, (("leaf", 1),), per_dev * leaf_size)
        window_points = window[:3].reshape(3, 3 * per_dev, leaf_size)
        window_vecs = window[3:].reshape(vec_count, 3 * per_dev, leaf_size)

        def near_slot(slot, running):
            chosen = lax.dynamic_index_in_dim(near_lists, slot, 1, keepdims=False)
            present = (chosen >= 0).astype(jnp.float32)
            safe_place = jnp.where(chosen >= 0, chosen, 0)
            source_points = jnp.take(window_points, safe_place, axis=1).transpose(1, 0, 2)
            source_vecs = jnp.take(window_vecs, safe_place, axis=1)
            kernel = matern(source_points, leaf_points)
            product = jnp.einsum("vlp,lpq->lvq", source_vecs, kernel, precision=highest)
            return running + present[:, None, None] * product

        near_part = lax.fori_loop(
            0, live_slots, near_slot, jnp.zeros((per_dev, vec_count, leaf_size), jnp.float32)
        )
        leaf_vecs = field.reshape(vec_count, per_dev, leaf_size)
        coeffs = jnp.einsum("vlp,lrp->lvr", leaf_vecs, interp, precision=highest)
        leaf_far = lax.psum_scatter(
            jnp.einsum("jvr,tjrq->tvq", coeffs, push_kernel, precision=highest),
            "leaf",
            scatter_dimension=0,
            tiled=True,
        )
        upward = jnp.einsum("lvr,lrc->vc", coeffs, transfer, precision=highest)
        subtree_total = lax.psum(upward, "leaf")
        group_coeffs = lax.all_gather(subtree_total[None], "grp", axis=0, tiled=True)
        coarse_field = jnp.einsum("avr,arq->vq", group_coeffs, coupling, precision=highest)
        downward = leaf_far + jnp.einsum("vc,lrc->lvr", coarse_field, transfer, precision=highest)
        far_part = jnp.einsum("lvr,lrp->lvp", downward, interp, precision=highest)
        combined = (near_part + far_part) / (leaf_size * slot_count)
        return combined.transpose(1, 0, 2).reshape(vec_count, per_dev * leaf_size)

    term_one = (operate(vectors) - centre * vectors) / half_width
    term_two = 2.0 * (operate(term_one) - centre * term_one) / half_width - vectors
    term_three = 2.0 * (operate(term_two) - centre * term_two) / half_width - term_one
    squares = lax.psum(jnp.sum(term_three * term_three, axis=1), ("grp", "leaf"))
    total_points = vectors.shape[1] * group_count * lax.axis_size("leaf")
    return term_three / jnp.sqrt(squares / total_points + 1e-06)[:, None]


def solution(mesh):
    placed = (
        P(None, ("grp", "leaf")),
        P(None, ("grp", "leaf")),
        P(("grp", "leaf"), None),
        P(("grp", "leaf"), None),
        P(("grp", "leaf"), None),
        P(("grp", "leaf"), None, None),
        P(("grp", "leaf"), None, None),
        P(),
    )
    return jax.shard_map(
        on_device, mesh=mesh, in_specs=placed, out_specs=P(None, ("grp", "leaf")), check_vma=False
    )
```

profile of v0, /device:TPU:10, one launch (start us, length us, event | category | flops | bytes accessed | tf_op | source)
XLA Modules:
  0.0 312.5 jit_solution(3287674258489741425)
XLA Ops:
  14.4 15.5 %all-gather = s32[16,2,16]{2,1,0:T(2,128)S(1)} all-gather(s32[1,2,16]{2,1,0:T(2,128)S(1)} %bitcast.260), channel_id=1, replica_groups=mesh['grp'=2,'leaf'=16] {'leaf'}, dimensions={0}, use_global_device_ids=true | all-gather | bytes 2176 | tf_op jit(solution)/shard_map/all_gather | solution.py:49
  30.1 21.1 %all_gather.15 = f32[32,3,64]{2,1,0:T(4,128)S(1)} all-gather(f32[2,3,64]{2,1,0:T(4,128)S(1)} %bitcast_select_fusion.1), channel_id=1, replica_groups=mesh['grp'=2,'leaf'=16] {'leaf'}, dimensions={0}, use_global_device_ids=true | all-gather | bytes 26112 | tf_op jit(solution)/shard_map/all_gather | solution.py:43
  51.6 3.5 %convolution_bitcast_fusion.2 = f32[32,16,64]{2,1,0:T(8,128)} fusion(f32[32,2]{1,0:T(8,128)S(1)} %copy.67, f32[32,64]{1,0:T(8,128)S(1)} %bitcast.254, f32[2,64]{1,0:T(2,128)S(1)} %bitcast.264, f32[32,64]{1,0:T(8,128)S(1)} %bitcast.257, f32[2,64]{1,0:T(2,128)S(1)} %bitcast.267, f32[32,64]{1,0:T(8,128)S(1)} %bitcast.251, f32[2,64]{1,0:T(2,128)S(1)} %bitcast.261, ...), kind=kOutput, calls=%fused_computation.145 | convolution fusion | flops 53739520 | bytes 165632 | tf_op jit(solution)/shard_map/jvr,tjrq->tvq/dot_general | solution.py:78
  56.1 24.3 %psum.28 = f32[1,16,128]{2,1,0:T(8,128)S(1)} all-reduce(f32[1,16,128]{2,1,0:T(8,128)S(1)} %convolution_bitcast_fusion.8), channel_id=1, replica_groups=mesh['grp'=2,'leaf'=16] {'leaf'}, use_global_device_ids=true, to_apply=%region_6.9 | all-reduce | flops 2048 | bytes 16384 | tf_op jit(solution)/shard_map/psum | solution.py:84
  80.4 4.4 %all_gather.17 = f32[2,16,128]{2,1,0:T(8,128)S(1)} all-gather(f32[1,16,128]{2,1,0:T(8,128)S(1)} %psum.28), channel_id=1, replica_groups=mesh['grp'=2,'leaf'=16] {'grp'}, dimensions={0}, use_global_device_ids=true | all-gather | bytes 24576 | tf_op jit(solution)/shard_map/all_gather | solution.py:85
  86.1 28.6 %while.30 = (s32[]{:T(128)}, f32[2,16,512]{2,1,0:T(8,128)S(1)}, s32[]{:T(128)}, s32[2,6]{0,1:T(8,128)S(1)}, f32[16,6,512]{2,0,1:T(8,128)S(1)}, /*index=5*/f32[3,...) while((s32[]{:T(128)}, f32[2,16,512]{2,1,0:T(8,128)S(1)}, s32[]{:T(128)}, ...), condition=%wide.region_3.0_spmd, body=%wide.region_2.0_spmd.sunk | while | flops 107008024 | bytes 479441 | solution.py:72
  87.9 2.8 fusion.199
  92.6 2.8 fusion.199
  97.3 2.8 fusion.199
  102.0 2.8 fusion.199
  106.6 2.8 fusion.199
  111.3 2.8 fusion.199
  120.7 3.5 %convolution_bitcast_fusion.1 = f32[32,16,64]{2,1,0:T(8,128)} fusion(f32[32,2]{1,0:T(8,128)S(1)} %copy.67, f32[32,64]{1,0:T(8,128)S(1)} %bitcast.255, f32[2,64]{1,0:T(2,128)S(1)} %bitcast.265, f32[32,64]{1,0:T(8,128)S(1)} %bitcast.258, f32[2,64]{1,0:T(2,128)S(1)} %bitcast.268, f32[32,64]{1,0:T(8,128)S(1)} %bitcast.252, f32[2,64]{1,0:T(2,128)S(1)} %bitcast.262, ...), kind=kOutput, calls=%fused_computation.144 | convolution fusion | flops 53739520 | bytes 165632 | tf_op jit(solution)/shard_map/jvr,tjrq->tvq/dot_general | solution.py:78
  124.4 26.7 %psum.29 = f32[1,16,128]{2,1,0:T(8,128)S(1)} all-reduce(f32[1,16,128]{2,1,0:T(8,128)S(1)} %convolution_bitcast_fusion.7), channel_id=1, replica_groups=mesh['grp'=2,'leaf'=16] {'leaf'}, use_global_device_ids=true, to_apply=%region_10.13 | all-reduce | flops 2048 | bytes 16384 | tf_op jit(solution)/shard_map/psum | solution.py:84
  151.2 4.4 %all_gather.18 = f32[2,16,128]{2,1,0:T(8,128)S(1)} all-gather(f32[1,16,128]{2,1,0:T(8,128)S(1)} %psum.29), channel_id=1, replica_groups=mesh['grp'=2,'leaf'=16] {'grp'}, dimensions={0}, use_global_device_ids=true | all-gather | bytes 24576 | tf_op jit(solution)/shard_map/all_gather | solution.py:85
  156.0 28.8 %while.31 = (s32[]{:T(128)}, f32[2,16,512]{2,1,0:T(8,128)S(1)}, s32[]{:T(128)}, s32[2,6]{0,1:T(8,128)S(1)}, f32[16,6,512]{2,0,1:T(8,128)S(1)}, /*index=5*/f32[3,...) while((s32[]{:T(128)}, f32[2,16,512]{2,1,0:T(8,128)S(1)}, s32[]{:T(128)}, ...), condition=%wide.region_8.11_spmd, body=%wide.region_7.10_spmd.sunk | while | flops 107008024 | bytes 479441 | solution.py:72
  158.1 2.8 fusion.203
  162.7 2.8 fusion.203
  176.8 2.8 fusion.203
  191.3 3.5 %convolution_bitcast_fusion = f32[32,16,64]{2,1,0:T(8,128)} fusion(f32[32,2]{1,0:T(8,128)S(1)} %copy.67, f32[32,64]{1,0:T(8,128)S(1)} %bitcast.256, f32[2,64]{1,0:T(2,128)S(1)} %bitcast.266, f32[32,64]{1,0:T(8,128)S(1)} %bitcast.259, f32[2,64]{1,0:T(2,128)S(1)} %bitcast.269, f32[32,64]{1,0:T(8,128)S(1)} %bitcast.253, f32[2,64]{1,0:T(2,128)S(1)} %bitcast.263, ...), kind=kOutput, calls=%fused_computation.143 | convolution fusion | flops 53739520 | bytes 165632 | tf_op jit(solution)/shard_map/jvr,tjrq->tvq/dot_general | solution.py:78
  195.0 28.1 %psum.30 = f32[1,16,128]{2,1,0:T(8,128)S(1)} all-reduce(f32[1,16,128]{2,1,0:T(8,128)S(1)} %convolution_bitcast_fusion.6), channel_id=1, replica_groups=mesh['grp'=2,'leaf'=16] {'leaf'}, use_global_device_ids=true, to_apply=%region_14.17 | all-reduce | flops 2048 | bytes 16384 | tf_op jit(solution)/shard_map/psum | solution.py:84
  223.1 4.4 %all_gather.19 = f32[2,16,128]{2,1,0:T(8,128)S(1)} all-gather(f32[1,16,128]{2,1,0:T(8,128)S(1)} %psum.30), channel_id=1, replica_groups=mesh['grp'=2,'leaf'=16] {'grp'}, dimensions={0}, use_global_device_ids=true | all-gather | bytes 24576 | tf_op jit(solution)/shard_map/all_gather | solution.py:85
  227.9 28.6 %while.32 = (s32[]{:T(128)}, f32[2,16,512]{2,1,0:T(8,128)S(1)}, s32[]{:T(128)}, s32[2,6]{0,1:T(8,128)S(1)}, f32[16,6,512]{2,0,1:T(8,128)S(1)}, /*index=5*/f32[3,...) while((s32[]{:T(128)}, f32[2,16,512]{2,1,0:T(8,128)S(1)}, s32[]{:T(128)}, ...), condition=%wide.region_12.15_spmd, body=%wide.region_11.14_spmd.sunk | while | flops 107008024 | bytes 479441 | solution.py:72
  258.7 46.5 %psum.31 = f32[16]{0:T(128)S(1)} all-reduce(f32[16]{0:T(128)S(1)} %multiply_reduce_fusion), channel_id=1, replica_groups=mesh['grp'=2,'leaf'=16] {'grp','leaf'}, use_global_device_ids=true, to_apply=%region_16.19 | all-reduce | flops 16 | bytes 128 | tf_op jit(solution)/shard_map/psum | solution.py:95
  (252 shorter events, 74.4 us)
Async XLA Ops:
  6.5 44.8 %copy-start = (f32[2,64,512]{2,1,0:T(8,128)S(1)}, f32[2,64,512]{2,1,0:T(8,128)}, u32[]{:S(2)}) copy-start(f32[2,64,512]{2,1,0:T(8,128)} %param.23) | copy-start | bytes 786436
  6.5 6.4 %copy-start.7 = (s32[2,64]{1,0:T(2,128)S(1)}, s32[2,64]{1,0:T(2,128)}, u32[]{:S(2)}) copy-start(s32[2,64]{1,0:T(2,128)} %param.22) | copy-start | bytes 1540
  6.5 7.8 %copy-start.5 = (s32[2,16]{1,0:T(2,128)S(1)}, s32[2,16]{1,0:T(2,128)}, u32[]{:S(2)}) copy-start(s32[2,16]{1,0:T(2,128)} %param.21) | copy-start | bytes 388
  6.5 108.2 %reduce-scatter.4.cloned.1.call-start = ((), (), s32[]{:S(2)}) async-start(), calls=%async_computation.3 | async-start | bytes 278528 | tf_op jit(solution)/shard_map/reduce_scatter | solution.py:77
  7.5 43.8 %copy-start.2 = (f32[16,1024]{1,0:T(8,128)S(1)}, f32[16,1024]{1,0:T(8,128)}, u32[]{:S(2)}) copy-start(f32[16,1024]{1,0:T(8,128)} %param.18) | copy-start | bytes 196612
  7.5 78.5 %collective-permute-start.1 = (f32[19,1024]{1,0:T(8,128)S(1)}, f32[19,1024]{1,0:T(8,128)S(1)}, u32[]{:S(2)}, u32[]{:S(2)}) collective-permute-start(f32[19,1024]{1,0:T(8,128)S(1)} %pad_maximum_fusion.3), channel_id=1, source_target_pairs={{1,0},{2,1},{3,2},{4,3},{5,4},{6,5},{7,6},{8,7},{9,8},{10,9},{11,1... | collective-permute-start | bytes 233480 | tf_op jit(solution)/shard_map/ppermute | solution.py:20
  9.5 76.4 %collective-permute-start = (f32[19,1024]{1,0:T(8,128)S(1)}, f32[19,1024]{1,0:T(8,128)S(1)}, u32[]{:S(2)}, u32[]{:S(2)}) collective-permute-start(f32[19,1024]{1,0:T(8,128)S(1)} %pad_maximum_fusion.3), channel_id=1, source_target_pairs={{0,1},{1,2},{2,3},{3,4},{4,5},{5,6},{6,7},{7,8},{8,9},{9,10},{10,1... | collective-permute-start | bytes 233480 | tf_op jit(solution)/shard_map/ppermute | solution.py:19
  55.1 0.7 copy-start.6
  55.1 0.9 copy-start.1
  55.1 29.7 %copy-start.4 = (f32[2,3,128]{2,0,1:T(2,128)S(1)}, f32[2,3,128]{2,0,1:T(2,128)}, u32[]{:S(2)}) copy-start(f32[2,3,128]{2,0,1:T(2,128)} %param.25) | copy-start | bytes 9220
  55.1 30.8 %copy-start.3 = (f32[3,1024]{1,0:T(4,128)S(1)}, f32[3,1024]{1,0:T(4,128)}, u32[]{:S(2)}) copy-start(f32[3,1024]{1,0:T(4,128)} %param.19) | copy-start | bytes 36868
  55.1 130.2 %reduce-scatter.6.cloned.1.call-start = ((), (), s32[]{:S(2)}) async-start(), calls=%async_computation.4 | async-start | bytes 278528 | tf_op jit(solution)/shard_map/reduce_scatter | solution.py:77
  116.0 39.9 %collective-permute-start.3 = (f32[19,1024]{1,0:T(8,128)S(1)}, f32[19,1024]{1,0:T(8,128)S(1)}, u32[]{:S(2)}, u32[]{:S(2)}) collective-permute-start(f32[19,1024]{1,0:T(8,128)S(1)} %pad_maximum_fusion.4), channel_id=1, source_target_pairs={{1,0},{2,1},{3,2},{4,3},{5,4},{6,5},{7,6},{8,7},{9,8},{10,9},{11,1... | collective-permute-start | bytes 233480 | tf_op jit(solution)/shard_map/ppermute | solution.py:20
  117.9 38.0 %collective-permute-start.2 = (f32[19,1024]{1,0:T(8,128)S(1)}, f32[19,1024]{1,0:T(8,128)S(1)}, u32[]{:S(2)}, u32[]{:S(2)}) collective-permute-start(f32[19,1024]{1,0:T(8,128)S(1)} %pad_maximum_fusion.4), channel_id=1, source_target_pairs={{0,1},{1,2},{2,3},{3,4},{4,5},{5,6},{6,7},{7,8},{8,9},{9,10},{10,1... | collective-permute-start | bytes 233480 | tf_op jit(solution)/shard_map/ppermute | solution.py:19
  124.4 132.9 %reduce-scatter.8.cloned.1.call-start = ((), (), s32[]{:S(2)}) async-start(), calls=%async_computation.5 | async-start | bytes 278528 | tf_op jit(solution)/shard_map/reduce_scatter | solution.py:77
  186.6 41.2 %collective-permute-start.5 = (f32[19,1024]{1,0:T(8,128)S(1)}, f32[19,1024]{1,0:T(8,128)S(1)}, u32[]{:S(2)}, u32[]{:S(2)}) collective-permute-start(f32[19,1024]{1,0:T(8,128)S(1)} %pad_maximum_fusion.5), channel_id=1, source_target_pairs={{1,0},{2,1},{3,2},{4,3},{5,4},{6,5},{7,6},{8,7},{9,8},{10,9},{11,1... | collective-permute-start | bytes 233480 | tf_op jit(solution)/shard_map/ppermute | solution.py:20
  188.5 39.3 %collective-permute-start.4 = (f32[19,1024]{1,0:T(8,128)S(1)}, f32[19,1024]{1,0:T(8,128)S(1)}, u32[]{:S(2)}, u32[]{:S(2)}) collective-permute-start(f32[19,1024]{1,0:T(8,128)S(1)} %pad_maximum_fusion.5), channel_id=1, source_target_pairs={{0,1},{1,2},{2,3},{3,4},{4,5},{5,6},{6,7},{7,8},{8,9},{9,10},{10,1... | collective-permute-start | bytes 233480 | tf_op jit(solution)/shard_map/ppermute | solution.py:19
Sparse Core Ops, SparseCore 0:
  55.2 56.6 reduce-scatter.3
  124.5 60.7 reduce-scatter.5
  195.1 62.1 reduce-scatter.7
where the time goes:
time: 313 us; the launch traced here: 312 us
  blocking collectives  175 us (56%)
  matrix products  66.6 us (21%)
  local copies, waits for them, and re-layouts  24.2 us (8%)
  loops' own time  13.7 us (4%)
  between operations  13.7 us (4%)
  starting transfers between devices  13.2 us (4%)
  other arithmetic  4.5 us (1%)
    psum x3, blocking collectives, operate(): subtree_total = lax.psum(upward, 'leaf')  79.1 us
    dot_general x18, matrix products, near_slot(): product = jnp.einsum('vlp,lpq->lvq', source_vecs, kernel, precision=highest)  50 us
    psum x1, blocking collectives, on_device(): lax.psum(jnp.sum(term_three * term_three, axis=1), ('grp', 'leaf'))  46.5 us
    all_gather x1, blocking collectives, on_device(): subtree_skel = lax.all_gather(skel_points, 'leaf', axis=0, tiled=True)  21.1 us
    all_gather x1, blocking collectives, on_device(): subtree_lists = lax.all_gather(inter_lists, 'leaf', axis=0, tiled=True)  15.5 us
    another operation x3, loops' own time, operate(): lax.fori_loop(0, live_slots, near_slot, jnp.zeros((per_dev, vec_count, le...  13.7 us
    all_gather x3, blocking collectives, operate(): lax.all_gather(subtree_total[None], 'grp', axis=0, tiled=True)  13.1 us
    dot_general x3, matrix products, operate(): jnp.einsum('jvr,tjrq->tvq', coeffs, push_kernel, precision=highest)  10.4 us
  transfers between devices with their start and end apart: 9, of which 2 were waited for; matrix products, arithmetic and copies ran while one was open for 29% of the time, Pallas kernels for 0%

commit v1 on v0

--- a/solution.py
+++ b/solution.py
@@ -92,7 +92,7 @@
     term_one = (operate(vectors) - centre * vectors) / half_width
     term_two = 2.0 * (operate(term_one) - centre * term_one) / half_width - vectors
     term_three = 2.0 * (operate(term_two) - centre * term_two) / half_width - term_one
-    squares = lax.psum(jnp.sum(term_three * term_three, axis=1), ("grp", "leaf"))
+    squares = lax.psum(lax.psum(jnp.sum(term_three * term_three, axis=1), "leaf"), "grp")
     total_points = vectors.shape[1] * group_count * lax.axis_size("leaf")
     return term_three / jnp.sqrt(squares / total_points + 1e-06)[:, None]
 

time: 313 us -> 312 us (level)
  the two profiles are of different devices: /device:TPU:10 before, /device:TPU:0 now
where the time goes in v1:
time: 312 us; the launch traced here: 311 us
  blocking collectives  190 us (61%)
  matrix products  49.9 us (16%)
  starting transfers between devices  25.4 us (8%)
  local copies, waits for them, and re-layouts  17.3 us (6%)
  between operations  13.7 us (4%)
  loops' own time  10.5 us (3%)
  other arithmetic  3.99 us (1%)
    psum x3, blocking collectives, operate(): subtree_total = lax.psum(upward, 'leaf')  95.2 us
    psum x1, blocking collectives, on_device(): lax.psum(jnp.sum(term_three * term_three, axis=1), 'leaf')  36.2 us
    dot_general x12, matrix products, near_slot(): product = jnp.einsum('vlp,lpq->lvq', source_vecs, kernel, precision=highest)  33.3 us
    all_gather x1, blocking collectives, on_device(): subtree_lists = lax.all_gather(inter_lists, 'leaf', axis=0, tiled=True)  23.1 us
    ppermute x3, starting transfers between devices, with_halo(): before = lax.ppermute(last, axis, up)  21.3 us
    all_gather x1, blocking collectives, on_device(): subtree_skel = lax.all_gather(skel_points, 'leaf', axis=0, tiled=True)  17.6 us
    all_gather x3, blocking collectives, operate(): lax.all_gather(subtree_total[None], 'grp', axis=0, tiled=True)  13.1 us
    another operation x3, loops' own time, operate(): lax.fori_loop(0, live_slots, near_slot, jnp.zeros((per_dev, vec_count, le...  10.5 us
  transfers between devices with their start and end apart: 9, of which 0 were waited for; matrix products, arithmetic and copies ran while one was open for 21% of the time, Pallas kernels for 0%

profile of v1, /device:TPU:0, one launch (start us, length us, event | category | flops | bytes accessed | tf_op | source)
XLA Modules:
  0.0 311.1 jit_solution(420931714834345022)
XLA Ops:
  8.9 3.0 collective-permute-start
  14.4 23.1 %all-gather = s32[16,2,16]{2,1,0:T(2,128)S(1)} all-gather(s32[1,2,16]{2,1,0:T(2,128)S(1)} %bitcast.260), channel_id=1, replica_groups=mesh['grp'=2,'leaf'=16] {'leaf'}, dimensions={0}, use_global_device_ids=true | all-gather | bytes 2176 | tf_op jit(solution)/shard_map/all_gather | solution.py:49
  37.7 17.6 %all_gather.15 = f32[32,3,64]{2,1,0:T(4,128)S(1)} all-gather(f32[2,3,64]{2,1,0:T(4,128)S(1)} %bitcast_select_fusion.1), channel_id=1, replica_groups=mesh['grp'=2,'leaf'=16] {'leaf'}, dimensions={0}, use_global_device_ids=true | all-gather | bytes 26112 | tf_op jit(solution)/shard_map/all_gather | solution.py:43
  55.7 3.5 %convolution_bitcast_fusion.2 = f32[32,16,64]{2,1,0:T(8,128)} fusion(f32[32,2]{1,0:T(8,128)S(1)} %copy.67, f32[32,64]{1,0:T(8,128)S(1)} %bitcast.254, f32[2,64]{1,0:T(2,128)S(1)} %bitcast.264, f32[32,64]{1,0:T(8,128)S(1)} %bitcast.257, f32[2,64]{1,0:T(2,128)S(1)} %bitcast.267, f32[32,64]{1,0:T(8,128)S(1)} %bitcast.251, f32[2,64]{1,0:T(2,128)S(1)} %bitcast.261, ...), kind=kOutput, calls=%fused_computation.145 | convolution fusion | flops 53739520 | bytes 165632 | tf_op jit(solution)/shard_map/jvr,tjrq->tvq/dot_general | solution.py:78
  60.2 31.6 %psum.35 = f32[1,16,128]{2,1,0:T(8,128)S(1)} all-reduce(f32[1,16,128]{2,1,0:T(8,128)S(1)} %convolution_bitcast_fusion.8), channel_id=1, replica_groups=mesh['grp'=2,'leaf'=16] {'leaf'}, use_global_device_ids=true, to_apply=%region_6.9 | all-reduce | flops 2048 | bytes 16384 | tf_op jit(solution)/shard_map/psum | solution.py:84
  91.9 4.4 %all_gather.17 = f32[2,16,128]{2,1,0:T(8,128)S(1)} all-gather(f32[1,16,128]{2,1,0:T(8,128)S(1)} %psum.35), channel_id=1, replica_groups=mesh['grp'=2,'leaf'=16] {'grp'}, dimensions={0}, use_global_device_ids=true | all-gather | bytes 24576 | tf_op jit(solution)/shard_map/all_gather | solution.py:85
  97.6 19.5 %while.30 = (s32[]{:T(128)}, f32[2,16,512]{2,1,0:T(8,128)S(1)}, s32[]{:T(128)}, s32[2,6]{0,1:T(8,128)S(1)}, f32[16,6,512]{2,0,1:T(8,128)S(1)}, /*index=5*/f32[3,...) while((s32[]{:T(128)}, f32[2,16,512]{2,1,0:T(8,128)S(1)}, s32[]{:T(128)}, ...), condition=%wide.region_3.0_spmd, body=%wide.region_2.0_spmd.sunk | while | flops 107008024 | bytes 479441 | solution.py:72
  99.5 2.8 fusion.199
  104.2 2.8 fusion.199
  108.9 2.8 fusion.199
  113.7 2.8 fusion.199
  119.7 9.0 %collective-permute-start.2 = (f32[19,1024]{1,0:T(8,128)S(1)}, f32[19,1024]{1,0:T(8,128)S(1)}, u32[]{:S(2)}, u32[]{:S(2)}) collective-permute-start(f32[19,1024]{1,0:T(8,128)S(1)} %pad_maximum_fusion.4), channel_id=1, source_target_pairs={{0,1},{1,2},{2,3},{3,4},{4,5},{5,6},{6,7},{7,8},{8,9},{9,10},{10,1... | collective-permute-start | bytes 233480 | tf_op jit(solution)/shard_map/ppermute | solution.py:19
  129.1 3.5 %convolution_bitcast_fusion.1 = f32[32,16,64]{2,1,0:T(8,128)} fusion(f32[32,2]{1,0:T(8,128)S(1)} %copy.67, f32[32,64]{1,0:T(8,128)S(1)} %bitcast.255, f32[2,64]{1,0:T(2,128)S(1)} %bitcast.265, f32[32,64]{1,0:T(8,128)S(1)} %bitcast.258, f32[2,64]{1,0:T(2,128)S(1)} %bitcast.268, f32[32,64]{1,0:T(8,128)S(1)} %bitcast.252, f32[2,64]{1,0:T(2,128)S(1)} %bitcast.262, ...), kind=kOutput, calls=%fused_computation.144 | convolution fusion | flops 53739520 | bytes 165632 | tf_op jit(solution)/shard_map/jvr,tjrq->tvq/dot_general | solution.py:78
  132.9 31.8 %psum.36 = f32[1,16,128]{2,1,0:T(8,128)S(1)} all-reduce(f32[1,16,128]{2,1,0:T(8,128)S(1)} %convolution_bitcast_fusion.7), channel_id=1, replica_groups=mesh['grp'=2,'leaf'=16] {'leaf'}, use_global_device_ids=true, to_apply=%region_10.13 | all-reduce | flops 2048 | bytes 16384 | tf_op jit(solution)/shard_map/psum | solution.py:84
  164.7 4.4 %all_gather.18 = f32[2,16,128]{2,1,0:T(8,128)S(1)} all-gather(f32[1,16,128]{2,1,0:T(8,128)S(1)} %psum.36), channel_id=1, replica_groups=mesh['grp'=2,'leaf'=16] {'grp'}, dimensions={0}, use_global_device_ids=true | all-gather | bytes 24576 | tf_op jit(solution)/shard_map/all_gather | solution.py:85
  169.5 19.7 %while.31 = (s32[]{:T(128)}, f32[2,16,512]{2,1,0:T(8,128)S(1)}, s32[]{:T(128)}, s32[2,6]{0,1:T(8,128)S(1)}, f32[16,6,512]{2,0,1:T(8,128)S(1)}, /*index=5*/f32[3,...) while((s32[]{:T(128)}, f32[2,16,512]{2,1,0:T(8,128)S(1)}, s32[]{:T(128)}, ...), condition=%wide.region_8.11_spmd, body=%wide.region_7.10_spmd.sunk | while | flops 107008024 | bytes 479441 | solution.py:72
  171.6 2.8 fusion.203
  191.9 9.2 %collective-permute-start.4 = (f32[19,1024]{1,0:T(8,128)S(1)}, f32[19,1024]{1,0:T(8,128)S(1)}, u32[]{:S(2)}, u32[]{:S(2)}) collective-permute-start(f32[19,1024]{1,0:T(8,128)S(1)} %pad_maximum_fusion.5), channel_id=1, source_target_pairs={{0,1},{1,2},{2,3},{3,4},{4,5},{5,6},{6,7},{7,8},{8,9},{9,10},{10,1... | collective-permute-start | bytes 233480 | tf_op jit(solution)/shard_map/ppermute | solution.py:19
  201.4 3.5 %convolution_bitcast_fusion = f32[32,16,64]{2,1,0:T(8,128)} fusion(f32[32,2]{1,0:T(8,128)S(1)} %copy.67, f32[32,64]{1,0:T(8,128)S(1)} %bitcast.256, f32[2,64]{1,0:T(2,128)S(1)} %bitcast.266, f32[32,64]{1,0:T(8,128)S(1)} %bitcast.259, f32[2,64]{1,0:T(2,128)S(1)} %bitcast.269, f32[32,64]{1,0:T(8,128)S(1)} %bitcast.253, f32[2,64]{1,0:T(2,128)S(1)} %bitcast.263, ...), kind=kOutput, calls=%fused_computation.143 | convolution fusion | flops 53739520 | bytes 165632 | tf_op jit(solution)/shard_map/jvr,tjrq->tvq/dot_general | solution.py:78
  205.1 31.8 %psum.37 = f32[1,16,128]{2,1,0:T(8,128)S(1)} all-reduce(f32[1,16,128]{2,1,0:T(8,128)S(1)} %convolution_bitcast_fusion.6), channel_id=1, replica_groups=mesh['grp'=2,'leaf'=16] {'leaf'}, use_global_device_ids=true, to_apply=%region_14.17 | all-reduce | flops 2048 | bytes 16384 | tf_op jit(solution)/shard_map/psum | solution.py:84
  237.0 4.4 %all_gather.19 = f32[2,16,128]{2,1,0:T(8,128)S(1)} all-gather(f32[1,16,128]{2,1,0:T(8,128)S(1)} %psum.37), channel_id=1, replica_groups=mesh['grp'=2,'leaf'=16] {'grp'}, dimensions={0}, use_global_device_ids=true | all-gather | bytes 24576 | tf_op jit(solution)/shard_map/all_gather | solution.py:85
  241.8 19.5 %while.32 = (s32[]{:T(128)}, f32[2,16,512]{2,1,0:T(8,128)S(1)}, s32[]{:T(128)}, s32[2,6]{0,1:T(8,128)S(1)}, f32[16,6,512]{2,0,1:T(8,128)S(1)}, /*index=5*/f32[3,...) while((s32[]{:T(128)}, f32[2,16,512]{2,1,0:T(8,128)S(1)}, s32[]{:T(128)}, ...), condition=%wide.region_12.15_spmd, body=%wide.region_11.14_spmd.sunk | while | flops 107008024 | bytes 479441 | solution.py:72
  262.8 36.2 %psum.38 = f32[16]{0:T(128)S(1)} all-reduce(f32[16]{0:T(128)S(1)} %multiply_reduce_fusion), channel_id=1, replica_groups=mesh['grp'=2,'leaf'=16] {'leaf'}, use_global_device_ids=true, to_apply=%region_16.19 | all-reduce | flops 16 | bytes 128 | tf_op jit(solution)/shard_map/psum | solution.py:95
  299.0 4.9 %psum.39 = f32[16]{0:T(128)S(1)} all-reduce(f32[16]{0:T(128)S(1)} %psum.38), channel_id=1, replica_groups=mesh['grp'=2,'leaf'=16] {'grp'}, use_global_device_ids=true, to_apply=%region_17.20 | all-reduce | flops 16 | bytes 128 | tf_op jit(solution)/shard_map/psum | solution.py:95
  (199 shorter events, 51.2 us)
Async XLA Ops:
  6.5 48.8 %copy-start = (f32[2,64,512]{2,1,0:T(8,128)S(1)}, f32[2,64,512]{2,1,0:T(8,128)}, u32[]{:S(2)}) copy-start(f32[2,64,512]{2,1,0:T(8,128)} %param.23) | copy-start | bytes 786436
  6.5 6.4 %copy-start.7 = (s32[2,64]{1,0:T(2,128)S(1)}, s32[2,64]{1,0:T(2,128)}, u32[]{:S(2)}) copy-start(s32[2,64]{1,0:T(2,128)} %param.22) | copy-start | bytes 1540
  6.5 7.8 %copy-start.5 = (s32[2,16]{1,0:T(2,128)S(1)}, s32[2,16]{1,0:T(2,128)}, u32[]{:S(2)}) copy-start(s32[2,16]{1,0:T(2,128)} %param.21) | copy-start | bytes 388
  6.5 110.6 %reduce-scatter.4.cloned.1.call-start = ((), (), s32[]{:S(2)}) async-start(), calls=%async_computation.3 | async-start | bytes 278528 | tf_op jit(solution)/shard_map/reduce_scatter | solution.py:77
  7.5 47.9 %copy-start.2 = (f32[16,1024]{1,0:T(8,128)S(1)}, f32[16,1024]{1,0:T(8,128)}, u32[]{:S(2)}) copy-start(f32[16,1024]{1,0:T(8,128)} %param.18) | copy-start | bytes 196612
  7.5 90.0 %collective-permute-start.1 = (f32[19,1024]{1,0:T(8,128)S(1)}, f32[19,1024]{1,0:T(8,128)S(1)}, u32[]{:S(2)}, u32[]{:S(2)}) collective-permute-start(f32[19,1024]{1,0:T(8,128)S(1)} %pad_maximum_fusion.3), channel_id=1, source_target_pairs={{1,0},{2,1},{3,2},{4,3},{5,4},{6,5},{7,6},{8,7},{9,8},{10,9},{11,1... | collective-permute-start | bytes 233480 | tf_op jit(solution)/shard_map/ppermute | solution.py:20
  8.9 88.5 %collective-permute-start = (f32[19,1024]{1,0:T(8,128)S(1)}, f32[19,1024]{1,0:T(8,128)S(1)}, u32[]{:S(2)}, u32[]{:S(2)}) collective-permute-start(f32[19,1024]{1,0:T(8,128)S(1)} %pad_maximum_fusion.3), channel_id=1, source_target_pairs={{0,1},{1,2},{2,3},{3,4},{4,5},{5,6},{6,7},{7,8},{8,9},{9,10},{10,1... | collective-permute-start | bytes 233480 | tf_op jit(solution)/shard_map/ppermute | solution.py:19
  59.2 0.7 copy-start.6
  59.2 0.9 copy-start.1
  59.2 37.1 %copy-start.4 = (f32[2,3,128]{2,0,1:T(2,128)S(1)}, f32[2,3,128]{2,0,1:T(2,128)}, u32[]{:S(2)}) copy-start(f32[2,3,128]{2,0,1:T(2,128)} %param.25) | copy-start | bytes 9220
  59.2 38.2 %copy-start.3 = (f32[3,1024]{1,0:T(4,128)S(1)}, f32[3,1024]{1,0:T(4,128)}, u32[]{:S(2)}) copy-start(f32[3,1024]{1,0:T(4,128)} %param.19) | copy-start | bytes 36868
  59.2 130.0 %reduce-scatter.6.cloned.1.call-start = ((), (), s32[]{:S(2)}) async-start(), calls=%async_computation.4 | async-start | bytes 278528 | tf_op jit(solution)/shard_map/reduce_scatter | solution.py:77
  118.4 51.0 %collective-permute-start.3 = (f32[19,1024]{1,0:T(8,128)S(1)}, f32[19,1024]{1,0:T(8,128)S(1)}, u32[]{:S(2)}, u32[]{:S(2)}) collective-permute-start(f32[19,1024]{1,0:T(8,128)S(1)} %pad_maximum_fusion.4), channel_id=1, source_target_pairs={{1,0},{2,1},{3,2},{4,3},{5,4},{6,5},{7,6},{8,7},{9,8},{10,9},{11,1... | collective-permute-start | bytes 233480 | tf_op jit(solution)/shard_map/ppermute | solution.py:20
  119.7 49.7 %collective-permute-start.2 = (f32[19,1024]{1,0:T(8,128)S(1)}, f32[19,1024]{1,0:T(8,128)S(1)}, u32[]{:S(2)}, u32[]{:S(2)}) collective-permute-start(f32[19,1024]{1,0:T(8,128)S(1)} %pad_maximum_fusion.4), channel_id=1, source_target_pairs={{0,1},{1,2},{2,3},{3,4},{4,5},{5,6},{6,7},{7,8},{8,9},{9,10},{10,1... | collective-permute-start | bytes 233480 | tf_op jit(solution)/shard_map/ppermute | solution.py:19
  132.8 128.6 %reduce-scatter.8.cloned.1.call-start = ((), (), s32[]{:S(2)}) async-start(), calls=%async_computation.5 | async-start | bytes 278528 | tf_op jit(solution)/shard_map/reduce_scatter | solution.py:77
  190.6 51.1 %collective-permute-start.5 = (f32[19,1024]{1,0:T(8,128)S(1)}, f32[19,1024]{1,0:T(8,128)S(1)}, u32[]{:S(2)}, u32[]{:S(2)}) collective-permute-start(f32[19,1024]{1,0:T(8,128)S(1)} %pad_maximum_fusion.5), channel_id=1, source_target_pairs={{1,0},{2,1},{3,2},{4,3},{5,4},{6,5},{7,6},{8,7},{9,8},{10,9},{11,1... | collective-permute-start | bytes 233480 | tf_op jit(solution)/shard_map/ppermute | solution.py:20
  191.9 49.8 %collective-permute-start.4 = (f32[19,1024]{1,0:T(8,128)S(1)}, f32[19,1024]{1,0:T(8,128)S(1)}, u32[]{:S(2)}, u32[]{:S(2)}) collective-permute-start(f32[19,1024]{1,0:T(8,128)S(1)} %pad_maximum_fusion.5), channel_id=1, source_target_pairs={{0,1},{1,2},{2,3},{3,4},{4,5},{5,6},{6,7},{7,8},{8,9},{9,10},{10,1... | collective-permute-start | bytes 233480 | tf_op jit(solution)/shard_map/ppermute | solution.py:19
Sparse Core Ops, SparseCore 0:
  59.3 54.1 reduce-scatter.3
  132.9 54.3 reduce-scatter.5
  205.3 54.3 reduce-scatter.7
